TPU v7x, 512 devices: a whole 4x8x8 slice. The times are simulated.
512 devices in a mesh: prow: 16 (over y, core), pcol: 32 (over z, x).
Axes of the slice: x: 4, y: 8, z: 8, core: 2. Of those that a mesh axis runs over, the one named last changes fastest.
Arguments:
- embeddings: bfloat16 [12, 16, 128, 768], P(None, 'prow', None, 'pcol'), may hold values from -6 to 6
- noise_var: bfloat16 [12, 16, 128], P(None, 'prow'), may hold values from 0.5 to 2
Outputs:
- schur_block: float32 [12, 16, 128, 6, 32, 128], P(None, 'prow', None, None, 'pcol')
- panel_cols: float32 [12, 16, 128, 128], P(None, 'prow', 'pcol')
All inputs are finite; a program needn't handle non-finite values.
Results may differ from a plain program's by a relative error of at most 0.0003.
Values may be sent and summed in bfloat16 or wider, within the bound.
A program may use at most 64 MiB of HBM per device.

v0:
```python
import jax
import jax.numpy as jnp
from jax import lax
from jax.sharding import PartitionSpec as P


def from_root(value, axis, source):
    kept = jnp.where(lax.axis_index(axis) == source, value, 0).astype(value.dtype)
    return lax.psum(kept, axis)


def squares(values):
    return jnp.sum(jnp.square(values.astype(jnp.float32)), axis=-1)


def kernel_block(left_x, right_x, left_sq, right_sq, feat_width):
    inner_dots = lax.dot_general(
        left_x, right_x, (((1,), (1,)), ((), ())), preferred_element_type=jnp.float32
    )
    return jnp.exp(-(left_sq[:, None] + right_sq[None, :] - 2.0 * inner_dots) / feat_width)


def shards(embeddings, noise_var):
    row_count = lax.axis_size("prow")
    col_count = lax.axis_size("pcol")
    row_index = lax.axis_index("prow")
    col_index = lax.axis_index("pcol")
    features = lax.all_gather(embeddings, "pcol", axis=3, tiled=True)
    row_tiles = features.shape[0]
    tile_size = features.shape[2]
    feat_width = features.shape[3]
    col_tiles = row_tiles * row_count // col_count
    group_ratio = col_count // row_count
    row_x = features.reshape(row_tiles * tile_size, feat_width)
    row_var = noise_var.reshape(row_tiles * tile_size).astype(jnp.float32)
    first_x, first_noise = (
        from_root(features[0, 0], "prow", 0),
        from_root(noise_var[0, 0], "prow", 0),
    )
    first_var = first_noise.astype(jnp.float32)
    grouped = features.reshape(col_tiles, group_ratio, tile_size, feat_width)
    chosen = lax.dynamic_index_in_dim(grouped, col_index // row_count, 1, keepdims=False)
    root_row = col_index % row_count
    col_x = from_root(chosen, "prow", root_row).reshape(col_tiles * tile_size, feat_width)
    row_sq = squares(row_x)
    col_sq = squares(col_x)
    first_sq = squares(first_x)
    offsets = jnp.arange(tile_size, dtype=jnp.int32)
    row_global = (
        (jnp.arange(row_tiles, dtype=jnp.int32) * row_count + row_index)[:, None] * tile_size
        + offsets[None, :]
    ).reshape(-1)
    col_global = (
        (jnp.arange(col_tiles, dtype=jnp.int32) * col_count + col_index)[:, None] * tile_size
        + offsets[None, :]
    ).reshape(-1)
    kernel_local = kernel_block(row_x, col_x, row_sq, col_sq, feat_width)
    kernel_local = kernel_local + jnp.where(
        row_global[:, None] == col_global[None, :], row_var[:, None], jnp.float32(0.0)
    )
    first_kernel = kernel_block(first_x, first_x, first_sq, first_sq, feat_width)
    first_kernel = first_kernel + jnp.where(
        offsets[:, None] == offsets[None, :], first_var[None, :], jnp.float32(0.0)
    )
    factor = jnp.linalg.cholesky(first_kernel)
    candidate = lax.linalg.triangular_solve(
        factor, kernel_local[:, :tile_size], left_side=False, lower=True, transpose_a=True
    )
    row_panel = from_root(candidate, "pcol", 0)
    regrouped = row_panel.reshape(col_tiles, group_ratio, tile_size, tile_size)
    picked = lax.dynamic_index_in_dim(regrouped, col_index // row_count, 1, keepdims=False)
    col_panel = from_root(picked, "prow", root_row).reshape(col_tiles * tile_size, tile_size)
    update = lax.dot_general(
        row_panel,
        col_panel,
        (((1,), (1,)), ((), ())),
        precision=lax.Precision.HIGHEST,
        preferred_element_type=jnp.float32,
    )
    schur_block = (kernel_local - update).reshape(row_tiles, 1, tile_size, col_tiles, 1, tile_size)
    share = tile_size // col_count
    panel_cols = lax.dynamic_slice_in_dim(
        row_panel.reshape(row_tiles, 1, tile_size, tile_size), col_index * share, share, 2
    )
    return (schur_block, panel_cols)


def solution(mesh):
    placed = (P(None, "prow", None, "pcol"), P(None, "prow", None))
    return jax.shard_map(
        shards,
        mesh=mesh,
        in_specs=placed,
        out_specs=(P(None, "prow", None, None, "pcol", None), P(None, "prow", "pcol", None)),
        check_vma=False,
    )
```

profile of v0, /device:TPU:1, one launch (start us, length us, event | category | flops | bytes accessed | tf_op | source)
XLA Modules:
  0.0 566.9 jit_solution(10739975928645798636)
XLA Ops:
  7.2 0.7 all-gather.2.cloned.1.call-update
  8.0 0.7 fusion.9
  8.7 29.8 %psum.37 = bf16[128]{0:T(256)(128)(2,1)S(1)} all-reduce(bf16[128]{0:T(256)(128)(2,1)S(1)} %fusion.9), channel_id=1, replica_groups=mesh['prow'=16,'pcol'=32] {'prow'}, use_global_device_ids=true, to_apply=%region_5.6 | all-reduce | flops 128 | bytes 512 | tf_op jit(solution)/shard_map/psum | solution.py:9
  38.5 0.1 add_bitcast_fusion
  38.6 57.0 %all-gather.2.cloned.1.call-done = bf16[12,1,128,768]{2,3,1,0:T(8,128)(2,1)} async-done(((bf16[12,1,128,24]{2,3,1,0:T(8,128)(2,1)}), bf16[12,1,128,768]{2,3,1,0:T(8,128)(2,1)}) %all-gather.2.cloned.1.call-update) | async-done | bytes 2359312 | tf_op jit(solution)/shard_map/all_gather | solution.py:28
  95.6 4.4 copy.23
  100.0 2.4 select_bitcast_fusion
  102.4 0.7 fusion.5
  103.2 0.1 add_bitcast_fusion.1
  103.2 0.5 multiply_reduce_fusion
  103.7 119.9 %all-reduce.9.cloned.1.call-done = (bf16[6,128,768]{2,1,0:T(8,128)(2,1)}, bf16[128,768]{0,1:T(8,128)(2,1)}) async-done(((bf16[6,128,768]{2,1,0:T(8,128)(2,1)}, bf16[128,768]{0,1:T(8,128)(2,1)}), (bf16[6,128,768]{2,1,0:T(8,128)(2,1)}, bf16[128,768]{0,1:T(8,128)(2,1)})) %all-reduce.9.cloned.1.call-update) | async-done | bytes 1376272 | tf_op jit(solution)/shard_map/psum | solution.py:9
  223.6 1.0 multiply_reduce_fusion.2
  224.6 1.3 broadcast_add_fusion
  225.9 0.1 copy.25
  226.0 1.6 multiply_reduce_fusion.1
  227.6 0.1 copy.26
  227.7 0.1 add_multiply_fusion
  227.8 11.7 %cholesky.16 = f32[128,128]{1,0:T(8,128)S(1)} custom-call(f32[128,128]{1,0:T(8,128)S(1)} %add_multiply_fusion), custom_call_target="Cholesky" | custom-call | tf_op jit(solution)/shard_map/jit(cholesky)/cholesky | solution.py:65
  239.5 0.6 compare_reduce_fusion
  240.2 0.7 fusion.6
  240.8 9.8 %custom-call.6 = f32[1,128,128]{1,2,0:T(8,128)S(1)} custom-call(f32[1,128,128]{2,1,0:T(8,128)S(1)} %fusion.6), custom_call_target="InvertDiagBlocksLowerTriangular" | custom-call | tf_op jit(solution)/shard_map/triangular_solve | solution.py:66
  250.6 4.6 fusion.3
  255.3 2.2 copy-done.1
  257.4 2.3 convolution_select_fusion
  259.8 0.2 all-reduce.7.cloned.1.call-start
  260.0 156.8 %all-reduce.5.cloned.1.call-done = f32[1536,128]{1,0:T(8,128)} async-done(((f32[1536,128]{1,0:T(8,128)}), f32[1536,128]{1,0:T(8,128)}) %all-reduce.5.cloned.1.call-update) | async-done | bytes 786448 | tf_op jit(solution)/shard_map/psum | solution.py:9
  416.8 1.8 dynamic-slice_select_fusion
  418.6 1.4 constant_dynamic-slice_fusion
  420.0 115.0 %all-reduce.7.cloned.1.call-done = f32[768,128]{1,0:T(8,128)} async-done(((f32[768,128]{1,0:T(8,128)}), f32[768,128]{1,0:T(8,128)}) %all-reduce.7.cloned.1.call-update) | async-done | bytes 393232 | tf_op jit(solution)/shard_map/psum | solution.py:9
  535.0 8.7 %convolution_subtract_fusion = f32[1536,768]{0,1:T(8,128)} fusion(f32[1536,768]{0,1:T(8,128)} %copy-done.1, f32[1536,128]{1,0:T(8,128)} %all-reduce.5.cloned.1.call-done, f32[768,128]{1,0:T(8,128)} %all-reduce.7.cloned.1.call-done), kind=kOutput, calls=%fused_computation.6 | convolution fusion | flops 1813118976 | bytes 10616832 | tf_op jit(solution)/shard_map/dot_general | solution.py:73
  543.8 6.7 %reshape.116 = f32[12,1,128,6,1,128]{2,0,5,3,4,1:T(8,128)} reshape(f32[1536,768]{0,1:T(8,128)} %convolution_subtract_fusion) | data formatting | bytes 9437184 | tf_op jit(solution)/shard_map/reshape | solution.py:80
  550.4 9.9 %copy.30 = f32[12,1,128,6,1,128]{5,4,3,2,1,0:T(1,128)} copy(f32[12,1,128,6,1,128]{2,0,5,3,4,1:T(8,128)} %reshape.116) | data formatting | bytes 9437184
  (16 shorter events, 0.2 us)
Async XLA Ops:
  7.2 96.1 %copy-start.2 = (bf16[12,1,128]{2,0,1:T(8,128)(2,1)S(1)}, bf16[12,1,128]{2,0,1:T(8,128)(2,1)}, u32[]{:S(2)}) copy-start(bf16[12,1,128]{2,0,1:T(8,128)(2,1)} %param.3) | copy-start | bytes 9220
  7.2 88.4 %all-gather.2.cloned.1.call-start = ((), (), s32[]{:S(2)}) async-start(), calls=%async_computation | async-start | bytes 2433024 | tf_op jit(solution)/shard_map/all_gather | solution.py:28
  7.9 215.7 %all-reduce.9.cloned.1.call-start = ((), (), s32[]{:S(2)}) async-start(), calls=%async_computation.3 | async-start | bytes 2752512 | tf_op jit(solution)/shard_map/psum | solution.py:9
  95.6 6.8 %copy-start = (bf16[12,1,128,768]{2,3,1,0:T(8,128)(2,1)S(1)}, bf16[12,1,128,768]{2,3,1,0:T(8,128)(2,1)}, u32[]{:S(2)}) copy-start(bf16[12,1,128,768]{2,3,1,0:T(8,128)(2,1)} %all-gather.2.cloned.1.call-done) | copy-start | bytes 7077892
  103.1 313.7 %all-reduce.5.cloned.1.call-start = ((), (), s32[]{:S(2)}) async-start(), calls=%async_computation.1 | async-start | bytes 1572864 | tf_op jit(solution)/shard_map/psum | solution.py:9
  255.3 2.2 copy-start.1
  259.8 275.2 %all-reduce.7.cloned.1.call-start = ((), (), s32[]{:S(2)}) async-start(), calls=%async_computation.2 | async-start | bytes 786432 | tf_op jit(solution)/shard_map/psum | solution.py:9
Sparse Core Ops, SparseCore 0:
  11.1 84.4 all-gather.1
  103.2 120.3 all-reduce.8
  259.9 156.8 all-reduce.4
  418.9 116.0 all-reduce.6
where the time goes:
time: 568 us; the launch traced here: 567 us
  waiting for transfers between devices  449 us (79%)
  other arithmetic  31.8 us (6%)
  blocking collectives  29.8 us (5%)
  local copies, waits for them, and re-layouts  24.8 us (4%)
  matrix products  16.9 us (3%)
  between operations  13.9 us (2%)
    psum x3, waiting for transfers between devices, from_root(): return lax.psum(kept, axis)  392 us
    all_gather x1, waiting for transfers between devices, shards(): features = lax.all_gather(embeddings, 'pcol', axis=3, tiled=True)  57 us
    psum x1, blocking collectives, from_root(): return lax.psum(kept, axis)  29.8 us
    another operation x3, other arithmetic, shards(): factor = jnp.linalg.cholesky(first_kernel)  12.4 us
    unnamed x7, local copies, waits for them, and re-layouts  12.1 us
  transfers between devices with their start and end apart: 4, of which 4 were waited for; matrix products, arithmetic and copies ran while one was open for 0% of the time, Pallas kernels for 0%

commit v1 on v0

--- a/solution.py
+++ b/solution.py
@@ -25,7 +25,9 @@
     col_count = lax.axis_size("pcol")
     row_index = lax.axis_index("prow")
     col_index = lax.axis_index("pcol")
-    features = lax.all_gather(embeddings, "pcol", axis=3, tiled=True)
+    new = jnp.stack([embeddings] * lax.axis_size("pcol"), 0)
+    moved = lax.all_to_all(new, "pcol", 0, 0)
+    features = jnp.concatenate(moved, axis=3)
     row_tiles = features.shape[0]
     tile_size = features.shape[2]
     feat_width = features.shape[3]

time: 568 us -> 544 us (0.958)
  waiting for transfers between devices: 449 us -> 411 us
  starting transfers between devices: 0.34 us -> 14.1 us
  local copies, waits for them, and re-layouts: 24.8 us -> 32.6 us
    all_gather x1 -> x0, waiting for transfers between devices: 57 us -> none  [shards(): features = lax.all_gather(embeddings, 'pcol', axis=3, tiled=True)]
    all_to_all x0 -> x1, waiting for transfers between devices: none -> 28.3 us  [shards(): moved = lax.all_to_all(new, 'pcol', 0, 0)]
    all_to_all x0 -> x1, starting transfers between devices: none -> 13.7 us  [shards(): moved = lax.all_to_all(new, 'pcol', 0, 0)]
    psum x3, waiting for transfers between devices: 392 us -> 383 us  [from_root(): return lax.psum(kept, axis)]
    reshape x0 -> x1, local copies, waits for them, and re-layouts: none -> 5.76 us  [shards(): features = jnp.concatenate(moved, axis=3)]
    unnamed x7 -> x9, local copies, waits for them, and re-layouts: 12.1 us -> 12.8 us
  transfers between devices with their start and end apart: 4 -> 4, of which waited for: 4 -> 4; matrix products, arithmetic and copies ran while one was open for 0% -> 1% of each run, Pallas kernels for 0% -> 0%
where the time goes in v1:
time: 544 us
  waiting for transfers between devices  411 us (76%)
  local copies, waits for them, and re-layouts  32.6 us (6%)
  other arithmetic  29.8 us (5%)
  blocking collectives  25.4 us (5%)
  matrix products  16.4 us (3%)
  starting transfers between devices  14.1 us (3%)
  between operations  13.9 us (3%)
    psum x3, waiting for transfers between devices, from_root(): return lax.psum(kept, axis)  383 us
    all_to_all x1, waiting for transfers between devices, shards(): moved = lax.all_to_all(new, 'pcol', 0, 0)  28.3 us
    psum x1, blocking collectives, from_root(): return lax.psum(kept, axis)  25.4 us
    all_to_all x1, starting transfers between devices, shards(): moved = lax.all_to_all(new, 'pcol', 0, 0)  13.7 us
    unnamed x9, local copies, waits for them, and re-layouts  12.8 us
    another operation x3, other arithmetic, shards(): factor = jnp.linalg.cholesky(first_kernel)  12.4 us
  transfers between devices with their start and end apart: 4, of which 4 were waited for; matrix products, arithmetic and copies ran while one was open for 1% of the time, Pallas kernels for 0%

profile of v1, /device:TPU:1, one launch (start us, length us, event | category | flops | bytes accessed | tf_op | source)
XLA Modules:
  0.0 543.5 jit_solution(4351422885183234728)
XLA Ops:
  7.2 2.6 stack.2
  9.8 13.7 %all-to-all-start = ((bf16[32,12,1,128,24]{3,4,1,2,0:T(8,128)(2,1)}), bf16[32,12,1,128,24]{3,4,1,2,0:T(8,128)(2,1)S(1)}, u32[]{:S(2)}, u32[]{:S(2)}) async-start(bf16[32,12,1,128,24]{3,4,1,2,0:T(8,128)(2,1)} %stack.2), calls=%async_computation | async-start | bytes 4718592 | tf_op jit(solution)/shard_map/all_to_all | solution.py:29
  23.6 25.4 %psum.37 = bf16[128]{0:T(256)(128)(2,1)S(1)} all-reduce(bf16[128]{0:T(256)(128)(2,1)S(1)} %fusion.10), channel_id=1, replica_groups=mesh['prow'=16,'pcol'=32] {'prow'}, use_global_device_ids=true, to_apply=%region_5.6 | all-reduce | flops 128 | bytes 512 | tf_op jit(solution)/shard_map/psum | solution.py:9
  49.1 28.3 %all-to-all-done = bf16[32,12,1,128,24]{3,4,1,2,0:T(8,128)(2,1)S(1)} async-done(((bf16[32,12,1,128,24]{3,4,1,2,0:T(8,128)(2,1)}), bf16[32,12,1,128,24]{3,4,1,2,0:T(8,128)(2,1)S(1)}, u32[]{:S(2)}, u32[]{:S(2)}) %all-to-all-start) | async-done | bytes 2359328 | tf_op jit(solution)/shard_map/all_to_all | solution.py:29
  77.4 0.5 copy.45
  78.0 0.7 slice_select_fusion
  78.7 0.7 copy-done
  79.4 1.1 select_bitcast_fusion
  80.7 5.8 %copy.27 = bf16[12,1,128,32,24]{2,0,4,3,1:T(8,128)(2,1)} copy(bf16[12,1,128,32,24]{2,4,3,0,1:T(8,128)(2,1)} %bitcast.62) | data formatting | bytes 4718592 | tf_op jit(solution)/shard_map/reshape | solution.py:30
  86.4 0.5 multiply_reduce_fusion
  86.9 111.3 %all-reduce.9.cloned.1.call-done = (bf16[6,128,768]{1,2,0:T(8,128)(2,1)}, bf16[128,768]{0,1:T(8,128)(2,1)}) async-done(((bf16[6,128,768]{1,2,0:T(8,128)(2,1)}, bf16[128,768]{0,1:T(8,128)(2,1)}), (bf16[6,128,768]{1,2,0:T(8,128)(2,1)}, bf16[128,768]{0,1:T(8,128)(2,1)})) %all-reduce.9.cloned.1.call-update) | async-done | bytes 1376272 | tf_op jit(solution)/shard_map/psum | solution.py:9
  198.2 1.5 multiply_reduce_fusion.1
  199.7 2.6 copy.26
  202.3 1.0 multiply_reduce_fusion.2
  203.3 1.3 broadcast_add_fusion
  204.7 0.1 copy.29
  204.8 0.1 add_multiply_fusion
  204.9 11.7 %cholesky.16 = f32[128,128]{1,0:T(8,128)S(1)} custom-call(f32[128,128]{1,0:T(8,128)S(1)} %add_multiply_fusion), custom_call_target="Cholesky" | custom-call | tf_op jit(solution)/shard_map/jit(cholesky)/cholesky | solution.py:67
  216.6 0.6 compare_reduce_fusion
  217.3 0.7 fusion.7
  217.9 9.8 %custom-call.6 = f32[1,128,128]{1,2,0:T(8,128)S(1)} custom-call(f32[1,128,128]{2,1,0:T(8,128)S(1)} %fusion.7), custom_call_target="InvertDiagBlocksLowerTriangular" | custom-call | tf_op jit(solution)/shard_map/triangular_solve | solution.py:68
  227.8 4.0 fusion.3
  231.8 2.2 copy-done.1
  234.0 2.3 convolution_select_fusion
  236.3 0.3 all-reduce.7.cloned.1.call-start
  236.6 156.7 %all-reduce.5.cloned.1.call-done = f32[1536,128]{1,0:T(8,128)} async-done(((f32[1536,128]{1,0:T(8,128)}), f32[1536,128]{1,0:T(8,128)}) %all-reduce.5.cloned.1.call-update) | async-done | bytes 786448 | tf_op jit(solution)/shard_map/psum | solution.py:9
  393.3 1.8 dynamic-slice_select_fusion
  395.1 1.4 constant_dynamic-slice_fusion
  396.5 115.1 %all-reduce.7.cloned.1.call-done = f32[768,128]{1,0:T(8,128)} async-done(((f32[768,128]{1,0:T(8,128)}), f32[768,128]{1,0:T(8,128)}) %all-reduce.7.cloned.1.call-update) | async-done | bytes 393232 | tf_op jit(solution)/shard_map/psum | solution.py:9
  511.7 8.7 %convolution_subtract_fusion = f32[1536,768]{0,1:T(8,128)} fusion(f32[1536,768]{0,1:T(8,128)} %copy-done.1, f32[1536,128]{1,0:T(8,128)} %all-reduce.5.cloned.1.call-done, f32[768,128]{1,0:T(8,128)} %all-reduce.7.cloned.1.call-done), kind=kOutput, calls=%fused_computation.6 | convolution fusion | flops 1813118976 | bytes 10616832 | tf_op jit(solution)/shard_map/dot_general | solution.py:75
  520.4 6.7 %reshape.118 = f32[12,1,128,6,1,128]{2,0,5,3,4,1:T(8,128)} reshape(f32[1536,768]{0,1:T(8,128)} %convolution_subtract_fusion) | data formatting | bytes 9437184 | tf_op jit(solution)/shard_map/reshape | solution.py:82
  527.1 9.9 %copy.33 = f32[12,1,128,6,1,128]{5,4,3,2,1,0:T(1,128)} copy(f32[12,1,128,6,1,128]{2,0,5,3,4,1:T(8,128)} %reshape.118) | data formatting | bytes 9437184
  (20 shorter events, 0.4 us)
Async XLA Ops:
  7.2 16.4 %copy-start.3 = (bf16[12,1,128]{2,0,1:T(8,128)(2,1)S(1)}, bf16[12,1,128]{2,0,1:T(8,128)(2,1)}, u32[]{:S(2)}) copy-start(bf16[12,1,128]{2,0,1:T(8,128)(2,1)} %param.3) | copy-start | bytes 9220
  9.8 67.6 %all-to-all-start = ((bf16[32,12,1,128,24]{3,4,1,2,0:T(8,128)(2,1)}), bf16[32,12,1,128,24]{3,4,1,2,0:T(8,128)(2,1)S(1)}, u32[]{:S(2)}, u32[]{:S(2)}) async-start(bf16[32,12,1,128,24]{3,4,1,2,0:T(8,128)(2,1)} %stack.2), calls=%async_computation | async-start | bytes 4718592 | tf_op jit(solution)/shard_map/all_to_all | solution.py:29
  23.5 174.7 %all-reduce.9.cloned.1.call-start = ((), (), s32[]{:S(2)}) async-start(), calls=%async_computation.3 | async-start | bytes 2752512 | tf_op jit(solution)/shard_map/psum | solution.py:9
  77.9 1.5 copy-start
  80.5 312.8 %all-reduce.5.cloned.1.call-start = ((), (), s32[]{:S(2)}) async-start(), calls=%async_computation.1 | async-start | bytes 1572864 | tf_op jit(solution)/shard_map/psum | solution.py:9
  86.9 140.9 %copy-start.2 = (bf16[12,1,128,32,24]{2,0,4,3,1:T(8,128)(2,1)S(1)}, bf16[12,1,128,32,24]{2,0,4,3,1:T(8,128)(2,1)}, u32[]{:S(2)}) copy-start(bf16[12,1,128,32,24]{2,0,4,3,1:T(8,128)(2,1)} %copy.27) | copy-start | bytes 7077892
  231.8 2.2 copy-start.1
  236.3 275.3 %all-reduce.7.cloned.1.call-start = ((), (), s32[]{:S(2)}) async-start(), calls=%async_computation.2 | async-start | bytes 786432 | tf_op jit(solution)/shard_map/psum | solution.py:9
Sparse Core Ops, SparseCore 0:
  80.6 117.5 all-reduce.8
  236.5 156.7 all-reduce.4
  395.6 116.0 all-reduce.6
